TPU v7x, 256 devices: a whole 4x4x8 slice. The times are simulated.
256 devices in a mesh: lat: 8 (over x_hi, y), lon: 32 (over x_lo, z, core).
Axes of the slice: x: 4 (x_hi: 2, x_lo: 2; x = x_hi * 2 + x_lo), y: 4, z: 8, core: 2. Of those that a mesh axis runs over, the one named last changes fastest.
Arguments:
- sea_state: bfloat16 [64, 256, 4096], P(None, 'lat', 'lon'), may hold values from -60 to 60
- conv_kernel: bfloat16 [64, 49], replicated, may hold values from -0.875 to 0.875
- conv_bias: bfloat16 [64], replicated, may hold values from -3 to 3
- norm_gain: bfloat16 [64], replicated, may hold values from 0.25 to 1.75
- norm_shift: bfloat16 [64], replicated, may hold values from -3 to 3
- w_in: bfloat16 [64, 256], replicated, may hold values from -0.75 to 0.75
- b_in: bfloat16 [256], replicated, may hold values from -3 to 3
- w_out: bfloat16 [256, 64], replicated, may hold values from -0.375 to 0.375
- b_out: bfloat16 [64], replicated, may hold values from -3 to 3
- layer_scale: bfloat16 [64], replicated, may hold values from 0.29882812 to 1
- sea_mask: int32 [256, 4096], P('lat', 'lon'), may hold values 0 or 1
- cotangent: bfloat16 [64, 256, 4096], P(None, 'lat', 'lon'), may hold values from -6 to 6
Outputs:
- new_state: bfloat16 [64, 256, 4096], P(None, 'lat', 'lon')
- state_grad: bfloat16 [64, 256, 4096], P(None, 'lat', 'lon')
- kernel_grad: float32 [64, 49], replicated
- w_in_grad: float32 [64, 256], replicated
- w_out_grad: float32 [256, 64], replicated
- b_in_grad: float32 [256], replicated
- channel_grads: float32 [5, 64], replicated
Inputs may be any that keep to these rules, and one draw needn't show every extreme that they name: `sea_mask`: 1 marks an ocean cell, 0 land.
All inputs are finite; a program needn't handle non-finite values. No bound on the sum of `sea_mask` on one device may be relied on, other than what follows from the above.
Results may differ from a plain program's by a relative error of at most 0.0062.
Values sent between devices are 32-bit elements; how exact they have to be, the bound alone decides.
No kernel may reach another device: no remote copies, remote signals or barrier semaphores. Data moves between devices by JAX's collectives and lax.ppermute only.
A program may use at most 128 MiB of HBM per device.

v0:
```python
import math
import jax
import jax.numpy as jnp
from jax import lax
from jax.sharding import PartitionSpec as P

slope_coef = 0.044715
tanh_scale = math.sqrt(2.0 / math.pi)
ln_epsilon = 1e-06


def with_halo(value, sides, width, wrap):
    for axis, dim in sides:
        size, length = (lax.axis_size(axis), value.shape[dim])
        up = [(i, (i + 1) % size) for i in range(size if wrap else size - 1)]
        down = [(j, i) for i, j in up]
        last = lax.slice_in_dim(value, length - width, length, axis=dim)
        initial = lax.slice_in_dim(value, 0, width, axis=dim)
        before = lax.ppermute(last, axis, up)
        after = lax.ppermute(initial, axis, down)
        value = jnp.concatenate([before, value, after], axis=dim)
    return value


def depthwise(padded, conv_kernel, conv_bias, row_count, col_count):
    weights = conv_kernel.astype(jnp.float32)
    running = (
        jnp.zeros((padded.shape[0], row_count, col_count), jnp.float32)
        + conv_bias.astype(jnp.float32)[:, None, None]
    )
    for row_off in range(7):
        for col_off in range(7):
            window = padded[:, row_off : row_off + row_count, col_off : col_off + col_count]
            running = running + weights[:, 7 * row_off + col_off][:, None, None] * window
    return running


def kernel_grads(padded, conv_grad):
    row_count = conv_grad.shape[1]
    col_count = conv_grad.shape[2]
    columns = []
    for row_off in range(7):
        for col_off in range(7):
            window = padded[:, row_off : row_off + row_count, col_off : col_off + col_count]
            columns.append(jnp.sum(conv_grad * window, axis=(1, 2)))
    return jnp.stack(columns, axis=1)


def spread_back(conv_grad, conv_kernel):
    row_count = conv_grad.shape[1]
    col_count = conv_grad.shape[2]
    weights = conv_kernel.astype(jnp.float32)
    widened = jnp.pad(conv_grad, ((0, 0), (6, 6), (6, 6)))
    running = jnp.zeros((conv_grad.shape[0], row_count + 6, col_count + 6), jnp.float32)
    for row_off in range(7):
        for col_off in range(7):
            window = widened[
                :, 6 - row_off : 12 - row_off + row_count, 6 - col_off : 12 - col_off + col_count
            ]
            running = running + weights[:, 7 * row_off + col_off][:, None, None] * window
    return running


def pointwise(
    conv_out,
    sea_state,
    cotangent,
    sea_mask,
    norm_gain,
    norm_shift,
    w_in,
    b_in,
    w_out,
    b_out,
    layer_scale,
):
    chan_count = conv_out.shape[0]
    flat_conv = conv_out.reshape(chan_count, -1)
    centre = flat_conv - jnp.mean(flat_conv, axis=0, keepdims=True)
    inv_std = lax.rsqrt(jnp.mean(centre * centre, axis=0, keepdims=True) + ln_epsilon)
    unit_norm = centre * inv_std
    gain_col = norm_gain.astype(jnp.float32)[:, None]
    normed = (unit_norm * gain_col + norm_shift.astype(jnp.float32)[:, None]).astype(jnp.bfloat16)
    pre_act = (
        jnp.dot(w_in.T, normed, preferred_element_type=jnp.float32)
        + b_in.astype(jnp.float32)[:, None]
    )
    tangent = jnp.tanh(tanh_scale * (pre_act + slope_coef * pre_act * pre_act * pre_act))
    hidden = (0.5 * pre_act * (1.0 + tangent)).astype(jnp.bfloat16)
    mixed_out = (
        jnp.dot(w_out.T, hidden, preferred_element_type=jnp.float32)
        + b_out.astype(jnp.float32)[:, None]
    )
    ocean_mask = sea_mask.reshape(1, -1).astype(jnp.float32)
    scale_col = layer_scale.astype(jnp.float32)[:, None]
    state_flat = sea_state.reshape(chan_count, -1).astype(jnp.float32)
    new_state = (ocean_mask * (state_flat + scale_col * mixed_out)).astype(jnp.bfloat16)
    masked_cot = ocean_mask * cotangent.reshape(chan_count, -1).astype(jnp.float32)
    mixed_grad = (scale_col * masked_cot).astype(jnp.bfloat16)
    scale_sum = jnp.sum(masked_cot * mixed_out, axis=1)
    out_bias_sum = jnp.sum(mixed_grad.astype(jnp.float32), axis=1)
    cell_axes = (((1,), (1,)), ((), ()))
    out_weight_sum = lax.dot_general(
        hidden, mixed_grad, cell_axes, preferred_element_type=jnp.float32
    )
    hidden_grad = jnp.dot(w_out, mixed_grad, preferred_element_type=jnp.float32)
    gelu_slope = 0.5 * (1.0 + tangent) + 0.5 * pre_act * (1.0 - tangent * tangent) * tanh_scale * (
        1.0 + 3.0 * slope_coef * pre_act * pre_act
    )
    pre_grad = (hidden_grad * gelu_slope).astype(jnp.bfloat16)
    in_bias_sum = jnp.sum(pre_grad.astype(jnp.float32), axis=1)
    in_weight_sum = lax.dot_general(normed, pre_grad, cell_axes, preferred_element_type=jnp.float32)
    normed_grad = jnp.dot(w_in, pre_grad, preferred_element_type=jnp.float32)
    gain_sum = jnp.sum(normed_grad * unit_norm, axis=1)
    shift_sum = jnp.sum(normed_grad, axis=1)
    unit_grad = normed_grad * gain_col
    conv_grad = inv_std * (
        unit_grad
        - jnp.mean(unit_grad, axis=0, keepdims=True)
        - unit_norm * jnp.mean(unit_grad * unit_norm, axis=0, keepdims=True)
    )
    partial_sums = (
        scale_sum,
        out_bias_sum,
        out_weight_sum,
        in_bias_sum,
        in_weight_sum,
        gain_sum,
        shift_sum,
    )
    return (
        new_state.reshape(conv_out.shape),
        conv_grad.reshape(conv_out.shape),
        masked_cot.reshape(conv_out.shape),
        partial_sums,
    )


def lon_extend(values):
    return with_halo(values, (("lon", 2),), 3, True)


def lat_extend(values):
    return with_halo(values, (("lat", 1),), 3, False)


def fold_partner(top_rows):
    lon_count = lax.axis_size("lon")
    pieces = top_rows.reshape(lon_count, -1)
    scattered = lax.all_to_all(pieces, "lon", split_axis=0, concat_axis=0, tiled=True)
    collected = lax.all_to_all(scattered[::-1], "lon", split_axis=0, concat_axis=0, tiled=True)
    return collected.reshape(top_rows.shape)


def fold_columns(values, col_count):
    col_rims = jnp.concatenate([values[:, :, :3], values[:, :, col_count + 3 :]], axis=2)
    col_from = lon_extend(col_rims)
    folded = values[:, :, 3 : col_count + 3]
    folded = folded.at[:, :, :3].add(col_from[:, :, :3])
    return folded.at[:, :, col_count - 3 :].add(col_from[:, :, 9:])


def fold_rows(values, row_count, on_top):
    row_rims = jnp.concatenate([values[:, :3], values[:, row_count + 3 :]], axis=1)
    row_from = lat_extend(row_rims)
    folded = values[:, 3 : row_count + 3]
    folded = folded.at[:, :3].add(row_from[:, :3])
    folded = folded.at[:, row_count - 3 :].add(row_from[:, 9:])
    returned = fold_partner(values[:, row_count + 3 :])[:, ::-1, ::-1]
    return folded.at[:, row_count - 3 :].add(jnp.where(on_top, returned, 0.0))


def per_device(
    sea_state,
    conv_kernel,
    conv_bias,
    norm_gain,
    norm_shift,
    w_in,
    b_in,
    w_out,
    b_out,
    layer_scale,
    sea_mask,
    cotangent,
):
    chan_count, row_count, col_count = sea_state.shape
    on_top = lax.axis_index("lat") == lax.axis_size("lat") - 1
    widened = sea_state.astype(jnp.float32)
    tall_field = lat_extend(widened)
    mirrored = fold_partner(widened[:, row_count - 3 :, :])[:, ::-1, ::-1]
    tall_field = jnp.concatenate(
        [
            tall_field[:, : row_count + 3],
            jnp.where(on_top, mirrored, tall_field[:, row_count + 3 :]),
        ],
        axis=1,
    )
    padded = lon_extend(tall_field)
    conv_out = depthwise(padded, conv_kernel, conv_bias, row_count, col_count)
    new_state, conv_grad, masked_cot, partial_sums = pointwise(
        conv_out,
        sea_state,
        cotangent,
        sea_mask,
        norm_gain,
        norm_shift,
        w_in,
        b_in,
        w_out,
        b_out,
        layer_scale,
    )
    scale_sum, out_bias_sum, out_weight_sum, in_bias_sum, in_weight_sum, gain_sum, shift_sum = (
        partial_sums
    )
    kernel_sum = kernel_grads(padded, conv_grad)
    bias_sum = jnp.sum(conv_grad, axis=(1, 2))
    spread = spread_back(conv_grad, conv_kernel)
    grid_grad = fold_rows(fold_columns(spread, col_count), row_count, on_top)
    state_grad = (masked_cot + grid_grad).astype(jnp.bfloat16)
    totals = lax.psum(
        (
            kernel_sum,
            bias_sum,
            gain_sum,
            shift_sum,
            out_bias_sum,
            scale_sum,
            in_weight_sum,
            out_weight_sum,
            in_bias_sum,
        ),
        ("lat", "lon"),
    )
    (
        kernel_total,
        bias_total,
        gain_total,
        shift_total,
        out_bias_total,
        scale_total,
        in_weight_total,
        out_weight_total,
        in_bias_total,
    ) = totals
    grad_scale = 1.0 / math.sqrt(
        row_count * lax.axis_size("lat") * col_count * lax.axis_size("lon")
    )
    channel_grads = grad_scale * jnp.stack(
        [bias_total, gain_total, shift_total, out_bias_total, scale_total]
    )
    return (
        new_state,
        state_grad,
        grad_scale * kernel_total,
        grad_scale * in_weight_total,
        grad_scale * out_weight_total,
        grad_scale * in_bias_total,
        channel_grads,
    )


def solution(mesh):
    placed = (
        P(None, "lat", "lon"),
        P(),
        P(),
        P(),
        P(),
        P(),
        P(),
        P(),
        P(),
        P(),
        P("lat", "lon"),
        P(None, "lat", "lon"),
    )
    return jax.shard_map(
        per_device,
        mesh=mesh,
        in_specs=placed,
        out_specs=(P(None, "lat", "lon"), P(None, "lat", "lon"), P(), P(), P(), P(), P()),
        check_vma=False,
    )
```

profile of v0, /device:TPU:1, one launch (start us, length us, event | category | flops | bytes accessed | tf_op | source)
XLA Modules:
  0.0 568.7 jit_solution(2259703244371274148)
XLA Ops:
  7.2 1.1 fusion.125
  8.3 4.0 collective-permute-start
  12.3 0.8 all_to_all.38
  13.1 10.5 %all-to-all-start = ((f32[32,1,768]{2,1,0:T(1,128)}), f32[32,1,768]{2,1,0:T(1,128)S(1)}, u32[]{:S(2)}, u32[]{:S(2)}) async-start(f32[32,1,768]{2,1,0:T(1,128)} %all_to_all.38), calls=%async_computation | async-start | bytes 196608 | tf_op jit(solution)/shard_map/all_to_all | solution.py:150
  23.6 1.3 collective-permute-start.1
  24.9 0.7 convert_element_type.89
  25.6 0.7 fusion.126
  26.3 2.2 bitcast_convert_fusion
  28.5 0.6 slice_bitcast_fusion.48
  29.2 2.8 all-to-all-done
  32.1 0.7 copy.20
  32.8 5.6 all-to-all-start.1
  38.4 0.7 slice_bitcast_fusion.47
  39.3 7.5 %all-to-all-done.1 = f32[32,1,768]{2,1,0:T(1,128)S(1)} async-done(((f32[32,1,768]{2,1,0:T(1,128)}), f32[32,1,768]{2,1,0:T(1,128)S(1)}, u32[]{:S(2)}, u32[]{:S(2)}) %all-to-all-start.1) | async-done | bytes 98336 | tf_op jit(solution)/shard_map/all_to_all | solution.py:151
  47.6 1.5 fusion.124
  49.1 1.8 copy.21
  50.9 1.9 collective-permute-start.2
  53.4 0.6 slice_bitcast_fusion.46
  56.2 1.6 copy.22
  57.8 1.6 copy.24
  59.4 5.1 maximum_maximum_fusion
  64.6 37.4 %fusion.121 = (f32[32,128]{1,0:T(8,128)S(1)}, f32[64,32,128]{2,1,0:T(8,128)}) fusion(f32[64,38,131]{2,1,0:T(8,128)} %get-tuple-element.148, f32[64]{0:T(128)S(1)} %get-tuple-element.158, f32[64]{0:T(128)S(1)} %get-tuple-element.159, f32[64]{0:T(128)S(1)} %get-tuple-element.160, f32[64,3,128]{2,1,0:T(4,128)S(1)} %broadcast_select_fusion, ...), kind=kLoop, calls=%fused_computation.319 | loop fusion | flops 27521024 | bytes 46363136 | tf_op jit(solution)/shard_map/reduce_sum | solution.py:79
  102.0 1.4 multiply_reduce_fusion.51
  103.4 4.7 multiply_convert_fusion
  108.1 4.5 convert_reduce_fusion
  112.6 1.0 fusion.114
  113.6 1.8 fusion.113
  115.7 8.1 %multiply_reduce_fusion.5 = (f32[64]{0:T(128)}, f32[64]{0:T(128)}, f32[64]{0:T(128)}, f32[64]{0:T(128)}, f32[64]{0:T(128)}, /*index=5*/f32[64]{0:T(128)}, f32[64...) fusion(f32[64,38,131]{2,1,0:T(8,128)S(1)} %get-tuple-element.14, ...), kind=kLoop, calls=%fused_computation.195 | loop fusion | flops 9436032 | bytes 19927552 | tf_op jit(solution)/shard_map/reduce_sum | solution.py:45
  124.2 28.6 %multiply_reduce_fusion.1 = (f32[64]{0:T(128)}, f32[64]{0:T(128)}, f32[64]{0:T(128)}, f32[64]{0:T(128)}, f32[64]{0:T(128)}, /*index=5*/f32[64]{0:T(128)}, f32[64...) fusion(f32[64,38,131]{2,1,0:T(8,128)} %get-tuple-element.148, ...), kind=kLoop, calls=%fused_computation.191 | loop fusion | flops 9436032 | bytes 19927552 | tf_op jit(solution)/shard_map/reduce_sum | solution.py:45
  152.8 1.1 multiply_reduce_fusion.25
  154.3 35.2 %fusion.104 = f32[64,38,134]{2,1,0:T(8,128)S(1)} fusion(f32[64,32,128]{2,1,0:T(8,128)S(1)} %bitcast.300, f32[64]{0:T(128)S(1)} %get-tuple-element.158, f32[64]{0:T(128)S(1)} %copy-done.14, f32[64]{0:T(128)S(1)} %copy-done.16, f32[64]{0:T(128)S(1)} %copy-done.18, f32[64]{0:T(128)S(1)} %copy-done.20, f32[64]{0:T(128)S(1)} %copy-done.22, f32[64]{0:T(128)S(1)} %copy-done.24, ...), kind=kLoop, calls=%fused_computation.160 | loop fusion | flops 31611136 | bytes 2364672 | tf_op jit(solution)/shard_map/add | solution.py:60
  189.5 2.7 fusion.122
  192.2 1.5 slice.995
  193.6 1.5 fusion.120
  195.2 2.4 copy.25
  197.6 1.7 collective-permute-start.4
  199.3 1.8 copy.26
  201.1 2.4 copy.28
  203.5 1.9 collective-permute-start.5
  205.3 1.9 reduce_sum.587
  207.2 3.4 fusion.117
  210.6 4.4 multiply_reduce_fusion
  215.0 0.9 copy.37
  216.3 9.0 %multiply_reduce_fusion.4 = (f32[64]{0:T(128)S(1)}, f32[64]{0:T(128)S(1)}, f32[64]{0:T(128)S(1)}, f32[64]{0:T(128)S(1)}, f32[64]{0:T(128)S(1)}, /*index=5*/f32[6...) fusion(f32[64,3,128]{2,1,0:T(4,128)S(1)} %broadcast_select_fusi, ...), kind=kLoop, calls=%fused_computation.194 | loop fusion | flops 7863552 | bytes 8588288 | tf_op jit(solution)/shard_map/reduce_sum | solution.py:45
  225.8 0.8 add.525
  227.2 7.1 %scatter-add.16 = f32[64,38,128]{2,1,0:T(8,128)} dynamic-update-slice(f32[64,38,128]{2,1,0:T(8,128)} %slice.995, f32[64,38,3]{2,1,0:T(8,128)S(1)} %copy.27, s32[]{:T(128)} %constant.160.clone.1, s32[]{:T(128)} %constant.160.clone.1, s32[]{:T(128)} %constant.160.clone.1) | dynamic-update-slice | bytes 58372 | tf_op jit(solution)/shard_map/scatter-add | solution.py:159
  234.3 1.8 slice.998
  236.6 0.9 add.526
  238.0 21.4 %scatter-add.19 = f32[64,38,128]{2,1,0:T(8,128)S(1)} dynamic-update-slice(f32[64,38,128]{2,1,0:T(8,128)S(1)} %copy-done.5, f32[64,38,3]{2,1,0:T(8,128)S(1)} %copy.30, s32[]{:T(128)} %constant.160.clone.1, s32[]{:T(128)} %constant.160.clone.1, s32[]{:T(128)} %constant.161.clone.1) | dynamic-update-slice | bytes 58372 | tf_op jit(solution)/shard_map/scatter-add | solution.py:160
  259.7 4.3 collective-permute-start.6
  263.9 0.8 all_to_all.39
  264.7 7.6 %all-to-all-start.2 = ((f32[32,1,768]{2,1,0:T(1,128)}), f32[32,1,768]{2,1,0:T(1,128)S(1)}, u32[]{:S(2)}, u32[]{:S(2)}) async-start(f32[32,1,768]{2,1,0:T(1,128)} %all_to_all.39), calls=%async_computation.2 | async-start | bytes 196608 | tf_op jit(solution)/shard_map/all_to_all | solution.py:150
  272.4 1.3 collective-permute-start.7
  273.7 188.9 %all-reduce.5.cloned.1.call-done = (f32[64,256]{1,0:T(8,128)}, f32[256,64]{0,1:T(8,128)}) async-done(((f32[64,256]{1,0:T(8,128)}, f32[256,64]{0,1:T(8,128)}), (f32[64,256]{1,0:T(8,128)}, f32[256,64]{0,1:T(8,128)})) %all-reduce.5.cloned.1.call-update) | async-done | bytes 131088 | tf_op jit(solution)/shard_map/psum | solution.py:222
  462.6 1.5 broadcast_multiply_fusion
  464.0 1.5 broadcast_multiply_fusion.1
  465.7 0.7 copy.32
  466.5 6.6 %all-to-all-start.3 = ((f32[32,1,768]{2,1,0:T(1,128)}), f32[32,1,768]{2,1,0:T(1,128)S(1)}, u32[]{:S(2)}, u32[]{:S(2)}) async-start(f32[32,1,768]{2,1,0:T(1,128)} %copy.32), calls=%async_computation.3 | async-start | bytes 196608 | tf_op jit(solution)/shard_map/all_to_all | solution.py:151
  473.6 7.9 %all-to-all-done.3 = f32[32,1,768]{2,1,0:T(1,128)S(1)} async-done(((f32[32,1,768]{2,1,0:T(1,128)}), f32[32,1,768]{2,1,0:T(1,128)S(1)}, u32[]{:S(2)}, u32[]{:S(2)}) %all-to-all-start.3) | async-done | bytes 98336 | tf_op jit(solution)/shard_map/all_to_all | solution.py:151
  482.0 1.0 select_add_fusion
  483.8 1.6 convert_reduce_fusion.1
  485.4 74.4 %all-reduce.1 = (f32[64,49]{0,1:T(8,128)S(1)}, f32[256]{0:T(256)S(1)}, f32[1,64]{1,0:T(1,128)S(1)}, f32[1,64]{1,0:T(1,128)S(1)}, f32[1,64]{1,0:T(1,128)S(1)}, /*index=5*/f32[1,64]{1,0:T(1,128)S(1)}, f32[1,64]{1,0:T(1,128)S(1)}) all-reduce(f32[64,49]{0,1:T(8,128)S(1)} %stack.217, ...), channel_id=1, replica_groups=mesh['lat'=8,'lon'=32] {'lat','lon'}, use_global_device_ids=true, to_apply=%region_53.54 | all-reduce | flops 3712 | bytes 29696 | tf_op jit(solution)/shard_map/psum | solution.py:222
  559.8 0.6 broadcast_multiply_fusion.6
  560.4 0.6 broadcast_multiply_fusion.2
  (278 shorter events, 8.9 us)
Async XLA Ops:
  7.2 96.2 %copy-start = (bf16[64,256]{1,0:T(8,128)(2,1)S(1)}, bf16[64,256]{1,0:T(8,128)(2,1)}, u32[]{:S(2)}) copy-start(bf16[64,256]{1,0:T(8,128)(2,1)} %param.27) | copy-start | bytes 98308
  7.2 31.9 %copy-start.10 = (bf16[64,32,128]{2,1,0:T(8,128)(2,1)S(1)}, bf16[64,32,128]{2,1,0:T(8,128)(2,1)}, u32[]{:S(2)}) copy-start(bf16[64,32,128]{2,1,0:T(8,128)(2,1)} %param.22) | copy-start | bytes 1572868
  8.3 39.1 %collective-permute-start = (f32[64,3,128]{2,1,0:T(4,128)S(1)}, f32[64,3,128]{2,1,0:T(4,128)S(1)}, u32[]{:S(2)}, u32[]{:S(2)}) collective-permute-start(f32[64,3,128]{2,1,0:T(4,128)S(1)} %get-tuple-element.156), channel_id=1, source_target_pairs={{0,32},{32,64},{64,96},{96,128},{128,160},{160,192},{192,224},{1,3... | collective-permute-start | bytes 294920 | tf_op jit(solution)/shard_map/ppermute | solution.py:19
  13.1 18.9 %all-to-all-start = ((f32[32,1,768]{2,1,0:T(1,128)}), f32[32,1,768]{2,1,0:T(1,128)S(1)}, u32[]{:S(2)}, u32[]{:S(2)}) async-start(f32[32,1,768]{2,1,0:T(1,128)} %all_to_all.38), calls=%async_computation | async-start | bytes 196608 | tf_op jit(solution)/shard_map/all_to_all | solution.py:150
  23.6 23.8 %collective-permute-start.1 = (f32[64,3,128]{2,1,0:T(4,128)S(1)}, f32[64,3,128]{2,1,0:T(4,128)S(1)}, u32[]{:S(2)}, u32[]{:S(2)}) collective-permute-start(f32[64,3,128]{2,1,0:T(4,128)S(1)} %get-tuple-element.155), channel_id=1, source_target_pairs={{32,0},{64,32},{96,64},{128,96},{160,128},{192,160},{224,192},{33,... | collective-permute-start | bytes 294920 | tf_op jit(solution)/shard_map/ppermute | solution.py:20
  29.1 35.4 %copy-start.13 = (f32[64]{0:T(128)}, f32[64]{0:T(128)S(1)}, u32[]{:S(2)}) copy-start(f32[64]{0:T(128)S(1)} %get-tuple-element.159) | copy-start | bytes 772
  29.1 35.4 %copy-start.15 = (f32[64]{0:T(128)}, f32[64]{0:T(128)S(1)}, u32[]{:S(2)}) copy-start(f32[64]{0:T(128)S(1)} %get-tuple-element.160) | copy-start | bytes 772
  29.1 35.4 %copy-start.17 = (f32[64]{0:T(128)}, f32[64]{0:T(128)S(1)}, u32[]{:S(2)}) copy-start(f32[64]{0:T(128)S(1)} %get-tuple-element.161) | copy-start | bytes 772
  29.1 35.4 %copy-start.19 = (f32[64]{0:T(128)}, f32[64]{0:T(128)S(1)}, u32[]{:S(2)}) copy-start(f32[64]{0:T(128)S(1)} %get-tuple-element.162) | copy-start | bytes 772
  29.1 35.4 %copy-start.21 = (f32[64]{0:T(128)}, f32[64]{0:T(128)S(1)}, u32[]{:S(2)}) copy-start(f32[64]{0:T(128)S(1)} %get-tuple-element.163) | copy-start | bytes 772
  29.1 35.4 %copy-start.23 = (f32[64]{0:T(128)}, f32[64]{0:T(128)S(1)}, u32[]{:S(2)}) copy-start(f32[64]{0:T(128)S(1)} %get-tuple-element.164) | copy-start | bytes 772
  29.1 35.4 %copy-start.25 = (f32[64]{0:T(128)}, f32[64]{0:T(128)S(1)}, u32[]{:S(2)}) copy-start(f32[64]{0:T(128)S(1)} %get-tuple-element.165) | copy-start | bytes 772
  29.1 35.4 %copy-start.27 = (f32[64]{0:T(128)}, f32[64]{0:T(128)S(1)}, u32[]{:S(2)}) copy-start(f32[64]{0:T(128)S(1)} %get-tuple-element.166) | copy-start | bytes 772
  29.2 35.4 %copy-start.29 = (f32[64]{0:T(128)}, f32[64]{0:T(128)S(1)}, u32[]{:S(2)}) copy-start(f32[64]{0:T(128)S(1)} %get-tuple-element.167) | copy-start | bytes 772
  32.8 13.9 %all-to-all-start.1 = ((f32[32,1,768]{2,1,0:T(1,128)}), f32[32,1,768]{2,1,0:T(1,128)S(1)}, u32[]{:S(2)}, u32[]{:S(2)}) async-start(f32[32,1,768]{2,1,0:T(1,128)} %copy.20), calls=%async_computation.1 | async-start | bytes 196608 | tf_op jit(solution)/shard_map/all_to_all | solution.py:151
  38.4 424.2 %all-reduce.5.cloned.1.call-start = ((), (), s32[]{:S(2)}) async-start(), calls=%async_computation.4 | async-start | bytes 262144 | tf_op jit(solution)/shard_map/psum | solution.py:222
  50.9 5.2 collective-permute-start.2
  53.3 4.4 collective-permute-start.3
  115.7 38.2 %copy-start.2 = (f32[8,8,32,128]{3,2,1,0:T(8,128)}, f32[8,8,32,128]{3,2,1,0:T(8,128)S(1)}, u32[]{:S(2)}) copy-start(f32[8,8,32,128]{3,2,1,0:T(8,128)S(1)} %copy.39) | copy-start | bytes 3145732
  123.8 30.1 %copy-start.18 = (f32[64]{0:T(128)S(1)}, f32[64]{0:T(128)}, u32[]{:S(2)}) copy-start(f32[64]{0:T(128)} %copy-done.17) | copy-start | bytes 772
  123.8 30.1 %copy-start.20 = (f32[64]{0:T(128)S(1)}, f32[64]{0:T(128)}, u32[]{:S(2)}) copy-start(f32[64]{0:T(128)} %copy-done.19) | copy-start | bytes 772
  123.8 30.1 %copy-start.22 = (f32[64]{0:T(128)S(1)}, f32[64]{0:T(128)}, u32[]{:S(2)}) copy-start(f32[64]{0:T(128)} %copy-done.21) | copy-start | bytes 772
  123.8 30.1 %copy-start.24 = (f32[64]{0:T(128)S(1)}, f32[64]{0:T(128)}, u32[]{:S(2)}) copy-start(f32[64]{0:T(128)} %copy-done.23) | copy-start | bytes 772
  123.8 30.1 %copy-start.26 = (f32[64]{0:T(128)S(1)}, f32[64]{0:T(128)}, u32[]{:S(2)}) copy-start(f32[64]{0:T(128)} %copy-done.25) | copy-start | bytes 772
  123.8 30.1 %copy-start.28 = (f32[64]{0:T(128)S(1)}, f32[64]{0:T(128)}, u32[]{:S(2)}) copy-start(f32[64]{0:T(128)} %copy-done.27) | copy-start | bytes 772
  123.8 30.1 %copy-start.30 = (f32[64]{0:T(128)S(1)}, f32[64]{0:T(128)}, u32[]{:S(2)}) copy-start(f32[64]{0:T(128)} %copy-done.29) | copy-start | bytes 772
  123.8 30.1 %copy-start.32 = (f32[64]{0:T(128)S(1)}, f32[64]{0:T(128)}, u32[]{:S(2)}) copy-start(f32[64]{0:T(128)} %get-tuple-element.168) | copy-start | bytes 772
  123.8 30.1 %copy-start.34 = (f32[64]{0:T(128)S(1)}, f32[64]{0:T(128)}, u32[]{:S(2)}) copy-start(f32[64]{0:T(128)} %get-tuple-element.169) | copy-start | bytes 772
  123.9 30.1 %copy-start.36 = (f32[64]{0:T(128)S(1)}, f32[64]{0:T(128)}, u32[]{:S(2)}) copy-start(f32[64]{0:T(128)} %get-tuple-element.170) | copy-start | bytes 772
  123.9 30.1 %copy-start.37 = (f32[64]{0:T(128)S(1)}, f32[64]{0:T(128)}, u32[]{:S(2)}) copy-start(f32[64]{0:T(128)} %get-tuple-element.171) | copy-start | bytes 772
  123.9 30.1 %copy-start.38 = (f32[64]{0:T(128)S(1)}, f32[64]{0:T(128)}, u32[]{:S(2)}) copy-start(f32[64]{0:T(128)} %get-tuple-element.172) | copy-start | bytes 772
  123.9 30.1 %copy-start.39 = (f32[64]{0:T(128)S(1)}, f32[64]{0:T(128)}, u32[]{:S(2)}) copy-start(f32[64]{0:T(128)} %get-tuple-element.173) | copy-start | bytes 772
  123.9 30.1 %copy-start.40 = (f32[64]{0:T(128)S(1)}, f32[64]{0:T(128)}, u32[]{:S(2)}) copy-start(f32[64]{0:T(128)} %get-tuple-element.174) | copy-start | bytes 772
  123.9 30.1 %copy-start.41 = (f32[64]{0:T(128)S(1)}, f32[64]{0:T(128)}, u32[]{:S(2)}) copy-start(f32[64]{0:T(128)} %get-tuple-element.175) | copy-start | bytes 772
  123.9 30.1 %copy-start.42 = (f32[64]{0:T(128)S(1)}, f32[64]{0:T(128)}, u32[]{:S(2)}) copy-start(f32[64]{0:T(128)} %get-tuple-element.176) | copy-start | bytes 772
  123.9 30.1 %copy-start.43 = (f32[64]{0:T(128)S(1)}, f32[64]{0:T(128)}, u32[]{:S(2)}) copy-start(f32[64]{0:T(128)} %get-tuple-element.177) | copy-start | bytes 772
  123.9 30.1 %copy-start.44 = (f32[64]{0:T(128)S(1)}, f32[64]{0:T(128)}, u32[]{:S(2)}) copy-start(f32[64]{0:T(128)} %get-tuple-element.178) | copy-start | bytes 772
  123.9 30.1 %copy-start.45 = (f32[64]{0:T(128)S(1)}, f32[64]{0:T(128)}, u32[]{:S(2)}) copy-start(f32[64]{0:T(128)} %get-tuple-element.179) | copy-start | bytes 772
  124.0 30.1 %copy-start.46 = (f32[64]{0:T(128)S(1)}, f32[64]{0:T(128)}, u32[]{:S(2)}) copy-start(f32[64]{0:T(128)} %get-tuple-element.180) | copy-start | bytes 772
  124.0 30.1 %copy-start.47 = (f32[64]{0:T(128)S(1)}, f32[64]{0:T(128)}, u32[]{:S(2)}) copy-start(f32[64]{0:T(128)} %get-tuple-element.181) | copy-start | bytes 772
  124.0 30.1 %copy-start.48 = (f32[64]{0:T(128)S(1)}, f32[64]{0:T(128)}, u32[]{:S(2)}) copy-start(f32[64]{0:T(128)} %get-tuple-element.182) | copy-start | bytes 772
  124.0 30.1 %copy-start.49 = (f32[64]{0:T(128)S(1)}, f32[64]{0:T(128)}, u32[]{:S(2)}) copy-start(f32[64]{0:T(128)} %get-tuple-element.183) | copy-start | bytes 772
  124.0 30.1 %copy-start.50 = (f32[64]{0:T(128)S(1)}, f32[64]{0:T(128)}, u32[]{:S(2)}) copy-start(f32[64]{0:T(128)} %get-tuple-element.184) | copy-start | bytes 772
  124.0 30.1 %copy-start.51 = (f32[64]{0:T(128)S(1)}, f32[64]{0:T(128)}, u32[]{:S(2)}) copy-start(f32[64]{0:T(128)} %get-tuple-element.185) | copy-start | bytes 772
  124.0 30.1 %copy-start.52 = (f32[64]{0:T(128)S(1)}, f32[64]{0:T(128)}, u32[]{:S(2)}) copy-start(f32[64]{0:T(128)} %get-tuple-element.186) | copy-start | bytes 772
  124.0 30.1 %copy-start.53 = (f32[64]{0:T(128)S(1)}, f32[64]{0:T(128)}, u32[]{:S(2)}) copy-start(f32[64]{0:T(128)} %get-tuple-element.187) | copy-start | bytes 772
  124.0 30.1 %copy-start.54 = (f32[64]{0:T(128)S(1)}, f32[64]{0:T(128)}, u32[]{:S(2)}) copy-start(f32[64]{0:T(128)} %get-tuple-element.188) | copy-start | bytes 772
  124.0 30.1 %copy-start.55 = (f32[64]{0:T(128)S(1)}, f32[64]{0:T(128)}, u32[]{:S(2)}) copy-start(f32[64]{0:T(128)} %get-tuple-element.189) | copy-start | bytes 772
  124.1 30.1 %copy-start.56 = (f32[64]{0:T(128)S(1)}, f32[64]{0:T(128)}, u32[]{:S(2)}) copy-start(f32[64]{0:T(128)} %get-tuple-element.190) | copy-start | bytes 772
  124.1 30.1 %copy-start.57 = (f32[64]{0:T(128)S(1)}, f32[64]{0:T(128)}, u32[]{:S(2)}) copy-start(f32[64]{0:T(128)} %get-tuple-element.191) | copy-start | bytes 772
  124.1 30.1 %copy-start.58 = (f32[64]{0:T(128)S(1)}, f32[64]{0:T(128)}, u32[]{:S(2)}) copy-start(f32[64]{0:T(128)} %get-tuple-element.192) | copy-start | bytes 772
  124.1 30.1 %copy-start.59 = (f32[64]{0:T(128)S(1)}, f32[64]{0:T(128)}, u32[]{:S(2)}) copy-start(f32[64]{0:T(128)} %get-tuple-element.193) | copy-start | bytes 772
  124.1 30.1 %copy-start.60 = (f32[64]{0:T(128)S(1)}, f32[64]{0:T(128)}, u32[]{:S(2)}) copy-start(f32[64]{0:T(128)} %get-tuple-element.194) | copy-start | bytes 772
  124.1 30.1 %copy-start.61 = (f32[64]{0:T(128)S(1)}, f32[64]{0:T(128)}, u32[]{:S(2)}) copy-start(f32[64]{0:T(128)} %get-tuple-element.195) | copy-start | bytes 772
  124.1 30.1 %copy-start.62 = (f32[64]{0:T(128)S(1)}, f32[64]{0:T(128)}, u32[]{:S(2)}) copy-start(f32[64]{0:T(128)} %get-tuple-element.196) | copy-start | bytes 772
  124.1 30.1 %copy-start.63 = (f32[64]{0:T(128)S(1)}, f32[64]{0:T(128)}, u32[]{:S(2)}) copy-start(f32[64]{0:T(128)} %get-tuple-element.197) | copy-start | bytes 772
  124.1 30.1 %copy-start.64 = (f32[64]{0:T(128)S(1)}, f32[64]{0:T(128)}, u32[]{:S(2)}) copy-start(f32[64]{0:T(128)} %get-tuple-element.198) | copy-start | bytes 772
  197.6 28.2 %collective-permute-start.4 = (f32[64,38,3]{0,1,2:T(8,128)}, f32[64,38,3]{0,1,2:T(8,128)}, u32[]{:S(2)}, u32[]{:S(2)}) collective-permute-start(f32[64,38,3]{0,1,2:T(8,128)} %copy.25), channel_id=1, source_target_pairs={{0,1},{1,2},{2,3},{3,4},{4,5},{5,6},{6,7},{7,8},{8,9},{9,10},{10,1... | collective-permute-start | bytes 87560 | tf_op jit(solution)/shard_map/ppermute | solution.py:19
  203.5 33.1 %collective-permute-start.5 = (f32[64,38,3]{0,1,2:T(8,128)}, f32[64,38,3]{0,1,2:T(8,128)}, u32[]{:S(2)}, u32[]{:S(2)}) collective-permute-start(f32[64,38,3]{0,1,2:T(8,128)} %copy.28), channel_id=1, source_target_pairs={{1,0},{2,1},{3,2},{4,3},{5,4},{6,5},{7,6},{8,7},{9,8},{10,9},{11,1... | collective-permute-start | bytes 87560 | tf_op jit(solution)/shard_map/ppermute | solution.py:20
  259.5 224.3 %copy-start.11 = (bf16[64,32,128]{2,1,0:T(8,128)(2,1)S(1)}, bf16[64,32,128]{2,1,0:T(8,128)(2,1)}, u32[]{:S(2)}) copy-start(bf16[64,32,128]{2,1,0:T(8,128)(2,1)} %param.33) | copy-start | bytes 1572868
  259.7 213.4 %collective-permute-start.6 = (f32[64,3,128]{2,1,0:T(4,128)S(1)}, f32[64,3,128]{2,1,0:T(4,128)S(1)}, u32[]{:S(2)}, u32[]{:S(2)}) collective-permute-start(f32[64,3,128]{2,1,0:T(4,128)S(1)} %get-tuple-element.146), channel_id=1, source_target_pairs={{0,32},{32,64},{64,96},{96,128},{128,160},{160,192},{192,224},{1,3... | collective-permute-start | bytes 294920 | tf_op jit(solution)/shard_map/ppermute | solution.py:19
  264.7 200.8 %all-to-all-start.2 = ((f32[32,1,768]{2,1,0:T(1,128)}), f32[32,1,768]{2,1,0:T(1,128)S(1)}, u32[]{:S(2)}, u32[]{:S(2)}) async-start(f32[32,1,768]{2,1,0:T(1,128)} %all_to_all.39), calls=%async_computation.2 | async-start | bytes 196608 | tf_op jit(solution)/shard_map/all_to_all | solution.py:150
  272.4 209.7 %collective-permute-start.7 = (f32[64,3,128]{2,1,0:T(4,128)S(1)}, f32[64,3,128]{2,1,0:T(4,128)}, u32[]{:S(2)}, u32[]{:S(2)}) collective-permute-start(f32[64,3,128]{2,1,0:T(4,128)S(1)} %get-tuple-element.145), channel_id=1, source_target_pairs={{32,0},{64,32},{96,64},{128,96},{160,128},{192,160},{224,192},{33,... | collective-permute-start | bytes 294920 | tf_op jit(solution)/shard_map/ppermute | solution.py:20
  466.5 15.0 %all-to-all-start.3 = ((f32[32,1,768]{2,1,0:T(1,128)}), f32[32,1,768]{2,1,0:T(1,128)S(1)}, u32[]{:S(2)}, u32[]{:S(2)}) async-start(f32[32,1,768]{2,1,0:T(1,128)} %copy.32), calls=%async_computation.3 | async-start | bytes 196608 | tf_op jit(solution)/shard_map/all_to_all | solution.py:151
  (64 other events, 605.8 us)
Sparse Core Ops, SparseCore 0:
  216.0 246.5 all-reduce.4
where the time goes:
time: 576 us; the launch traced here: 569 us
  waiting for transfers between devices  207 us (36%)
  other arithmetic  145 us (25%)
  blocking collectives  74.4 us (13%)
  local copies, waits for them, and re-layouts  59.6 us (10%)
  starting transfers between devices  46.8 us (8%)
  matrix products  19.5 us (3%)
  between operations  16.1 us (3%)
    psum x1, waiting for transfers between devices, per_device(): lax.psum((kernel_sum, bias_sum, gain_sum, shift_sum, out_bias_sum, scale_...  189 us
    psum x1, blocking collectives, per_device(): lax.psum((kernel_sum, bias_sum, gain_sum, shift_sum, out_bias_sum, scale_...  74.4 us
    reduce_sum x4, other arithmetic, kernel_grads(): columns.append(jnp.sum(conv_grad * window, axis=(1, 2)))  46.8 us
    reduce_sum x1, other arithmetic, pointwise(): centre = flat_conv - jnp.mean(flat_conv, axis=0, keepdims=True)  37.4 us
    add x1, other arithmetic, spread_back(): running + weights[:, 7 * row_off + col_off][:, None, None] * window  35.2 us
    scatter-add x1, local copies, waits for them, and re-layouts, fold_columns(): return folded.at[:, :, col_count - 3:].add(col_from[:, :, 9:])  21.4 us
    all_to_all x2, starting transfers between devices, fold_partner(): lax.all_to_all(pieces, 'lon', split_axis=0, concat_axis=0, tiled=True)  18.1 us
    all_to_all x2, waiting for transfers between devices, fold_partner(): lax.all_to_all(scattered[::-1], 'lon', split_axis=0, concat_axis=0, tiled...  15.3 us
  transfers between devices with their start and end apart: 13, of which 4 were waited for; matrix products, arithmetic and copies ran while one was open for 13% of the time, Pallas kernels for 0%

commit v1 on v0

--- a/solution.py
+++ b/solution.py
@@ -220,18 +220,21 @@
     grid_grad = fold_rows(fold_columns(spread, col_count), row_count, on_top)
     state_grad = (masked_cot + grid_grad).astype(jnp.bfloat16)
     totals = lax.psum(
-        (
-            kernel_sum,
-            bias_sum,
-            gain_sum,
-            shift_sum,
-            out_bias_sum,
-            scale_sum,
-            in_weight_sum,
-            out_weight_sum,
-            in_bias_sum,
+        lax.psum(
+            (
+                kernel_sum,
+                bias_sum,
+                gain_sum,
+                shift_sum,
+                out_bias_sum,
+                scale_sum,
+                in_weight_sum,
+                out_weight_sum,
+                in_bias_sum,
+            ),
+            "lat",
         ),
-        ("lat", "lon"),
+        "lon",
     )
     (
         kernel_total,

time: 576 us -> 675 us (1.17)
  blocking collectives: 74.4 us -> 142 us
  waiting for transfers between devices: 207 us -> 223 us
  starting transfers between devices: 46.8 us -> 54.4 us
    psum x0 -> x1, waiting for transfers between devices: none -> 194 us  [per_device(): lax.psum(lax.psum((kernel_sum, bias_sum, gain_sum, shift_sum, out_bias_su...]
    psum x1, waiting for transfers between devices: 189 us -> 18.1 us  [per_device(): lax.psum((kernel_sum, bias_sum, gain_sum, shift_sum, out_bias_sum, scale_...]
    psum x0 -> x1, blocking collectives: none -> 108 us  [per_device(): lax.psum(lax.psum((kernel_sum, bias_sum, gain_sum, shift_sum, out_bias_su...]
    psum x1, blocking collectives: 74.4 us -> 34.2 us  [per_device(): lax.psum((kernel_sum, bias_sum, gain_sum, shift_sum, out_bias_sum, scale_...]
    all_to_all x2, waiting for transfers between devices: 15.3 us -> 7.49 us  [fold_partner(): lax.all_to_all(scattered[::-1], 'lon', split_axis=0, concat_axis=0, tiled...]
  transfers between devices with their start and end apart: 13 -> 14, of which waited for: 4 -> 4; matrix products, arithmetic and copies ran while one was open for 13% -> 12% of each run, Pallas kernels for 0% -> 0%
where the time goes in v1:
time: 675 us; the launch traced here: 666 us
  waiting for transfers between devices  223 us (33%)
  other arithmetic  144 us (21%)
  blocking collectives  142 us (21%)
  local copies, waits for them, and re-layouts  65.5 us (10%)
  starting transfers between devices  54.4 us (8%)
  matrix products  21.4 us (3%)
  between operations  15.9 us (2%)
    psum x1, waiting for transfers between devices, per_device(): lax.psum(lax.psum((kernel_sum, bias_sum, gain_sum, shift_sum, out_bias_su...  194 us
    psum x1, blocking collectives, per_device(): lax.psum(lax.psum((kernel_sum, bias_sum, gain_sum, shift_sum, out_bias_su...  108 us
    reduce_sum x4, other arithmetic, kernel_grads(): columns.append(jnp.sum(conv_grad * window, axis=(1, 2)))  46.4 us
    reduce_sum x1, other arithmetic, pointwise(): centre = flat_conv - jnp.mean(flat_conv, axis=0, keepdims=True)  37.3 us
    add x1, other arithmetic, spread_back(): running + weights[:, 7 * row_off + col_off][:, None, None] * window  34.6 us
    psum x1, blocking collectives, per_device(): lax.psum((kernel_sum, bias_sum, gain_sum, shift_sum, out_bias_sum, scale_...  34.2 us
    all_to_all x2, starting transfers between devices, fold_partner(): lax.all_to_all(scattered[::-1], 'lon', split_axis=0, concat_axis=0, tiled...  18.9 us
    all_to_all x2, starting transfers between devices, fold_partner(): lax.all_to_all(pieces, 'lon', split_axis=0, concat_axis=0, tiled=True)  18.1 us
  transfers between devices with their start and end apart: 14, of which 4 were waited for; matrix products, arithmetic and copies ran while one was open for 12% of the time, Pallas kernels for 0%

profile of v1, /device:TPU:1, one launch (start us, length us, event | category | flops | bytes accessed | tf_op | source)
XLA Modules:
  0.0 665.7 jit_solution(13306825924163939246)
XLA Ops:
  7.2 1.1 fusion.125
  8.3 4.0 collective-permute-start
  12.3 0.8 all_to_all.38
  13.1 10.5 %all-to-all-start = ((f32[32,1,768]{2,1,0:T(1,128)}), f32[32,1,768]{2,1,0:T(1,128)S(1)}, u32[]{:S(2)}, u32[]{:S(2)}) async-start(f32[32,1,768]{2,1,0:T(1,128)} %all_to_all.38), calls=%async_computation | async-start | bytes 196608 | tf_op jit(solution)/shard_map/all_to_all | solution.py:150
  23.6 1.3 collective-permute-start.1
  24.9 0.7 convert_element_type.89
  25.6 0.7 fusion.126
  26.3 2.1 bitcast_convert_fusion
  29.0 2.9 all-to-all-done
  32.1 0.7 copy.20
  32.8 5.4 all-to-all-start.1
  38.2 0.7 slice_bitcast_fusion.47
  39.1 7.5 %all-to-all-done.1 = f32[32,1,768]{2,1,0:T(1,128)S(1)} async-done(((f32[32,1,768]{2,1,0:T(1,128)}), f32[32,1,768]{2,1,0:T(1,128)S(1)}, u32[]{:S(2)}, u32[]{:S(2)}) %all-to-all-start.1) | async-done | bytes 98336 | tf_op jit(solution)/shard_map/all_to_all | solution.py:151
  47.4 1.5 fusion.124
  48.9 1.8 copy.21
  50.8 1.9 collective-permute-start.2
  56.0 1.6 copy.22
  57.6 1.6 copy.24
  59.1 5.1 maximum_maximum_fusion
  64.2 37.3 %fusion.121 = (f32[32,128]{1,0:T(8,128)S(1)}, f32[64,32,128]{2,1,0:T(8,128)}) fusion(f32[64,38,131]{2,1,0:T(8,128)} %get-tuple-element.157, f32[64]{0:T(128)S(1)} %get-tuple-element.167, f32[64]{0:T(128)S(1)} %get-tuple-element.168, f32[64]{0:T(128)S(1)} %get-tuple-element.169, f32[64,3,128]{2,1,0:T(4,128)S(1)} %broadcast_select_fusion, ...), kind=kLoop, calls=%fused_computation.319 | loop fusion | flops 27521024 | bytes 46363136 | tf_op jit(solution)/shard_map/reduce_sum | solution.py:79
  101.6 1.4 multiply_reduce_fusion.51
  103.0 4.7 multiply_convert_fusion
  107.7 4.5 convert_reduce_fusion
  112.2 1.0 fusion.114
  113.3 1.8 fusion.113
  115.3 8.1 %multiply_reduce_fusion.5 = (f32[64]{0:T(128)}, f32[64]{0:T(128)}, f32[64]{0:T(128)}, f32[64]{0:T(128)}, f32[64]{0:T(128)}, /*index=5*/f32[64]{0:T(128)}, f32[64...) fusion(f32[64,38,131]{2,1,0:T(8,128)S(1)} %get-tuple-element.15, ...), kind=kLoop, calls=%fused_computation.195 | loop fusion | flops 9436032 | bytes 19927552 | tf_op jit(solution)/shard_map/reduce_sum | solution.py:45
  123.3 28.6 %multiply_reduce_fusion.1 = (f32[64]{0:T(128)}, f32[64]{0:T(128)}, f32[64]{0:T(128)}, f32[64]{0:T(128)}, f32[64]{0:T(128)}, /*index=5*/f32[64]{0:T(128)}, f32[64...) fusion(f32[64,38,131]{2,1,0:T(8,128)} %get-tuple-element.157, ...), kind=kLoop, calls=%fused_computation.191 | loop fusion | flops 9436032 | bytes 19927552 | tf_op jit(solution)/shard_map/reduce_sum | solution.py:45
  152.3 3.4 fusion.120
  156.0 34.6 %fusion.104 = f32[64,38,134]{2,1,0:T(8,128)S(1)} fusion(f32[64,32,128]{2,1,0:T(8,128)S(1)} %bitcast.300, f32[64]{0:T(128)S(1)} %get-tuple-element.167, f32[64]{0:T(128)S(1)} %get-tuple-element.168, f32[64]{0:T(128)S(1)} %get-tuple-element.169, f32[64]{0:T(128)S(1)} %get-tuple-element.170, f32[64]{0:T(128)S(1)} %get-tuple-element.171, ...), kind=kLoop, calls=%fused_computation.160 | loop fusion | flops 31611136 | bytes 2364672 | tf_op jit(solution)/shard_map/add | solution.py:60
  190.7 2.8 fusion.122
  193.5 2.4 copy.25
  195.9 1.7 collective-permute-start.4
  197.6 2.4 copy.28
  200.0 1.9 collective-permute-start.5
  201.9 1.9 reduce_sum.587
  203.8 3.4 fusion.117
  207.1 4.4 multiply_reduce_fusion
  211.5 0.9 copy.37
  212.4 9.1 %multiply_reduce_fusion.4 = (f32[64]{0:T(128)}, f32[64]{0:T(128)}, f32[64]{0:T(128)}, f32[64]{0:T(128)}, f32[64]{0:T(128)}, /*index=5*/f32[64]{0:T(128)}, f32[64...) fusion(f32[64,3,128]{2,1,0:T(4,128)S(1)} %broadcast_select_fusion, ...), kind=kLoop, calls=%fused_computation.194 | loop fusion | flops 7863552 | bytes 8588288 | tf_op jit(solution)/shard_map/reduce_sum | solution.py:45
  221.9 1.8 copy.26
  223.7 0.8 add.543
  224.6 1.5 copy.27
  226.1 11.2 %scatter-add.16 = f32[64,38,128]{2,1,0:T(8,128)S(1)} dynamic-update-slice(f32[64,38,128]{2,1,0:T(8,128)S(1)} %slice.995, f32[64,38,3]{2,1,0:T(8,128)} %copy.27, s32[]{:T(128)} %constant.160.clone.1, s32[]{:T(128)} %constant.160.clone.1, s32[]{:T(128)} %constant.160.clone.1) | dynamic-update-slice | bytes 58372 | tf_op jit(solution)/shard_map/scatter-add | solution.py:159
  237.3 1.5 slice.998
  238.8 1.8 copy.29
  240.6 1.5 copy.30
  242.5 18.0 %scatter-add.19 = f32[64,38,128]{2,1,0:T(8,128)S(1)} dynamic-update-slice(f32[64,38,128]{2,1,0:T(8,128)S(1)} %scatter-add.16, f32[64,38,3]{2,1,0:T(8,128)} %copy.30, s32[]{:T(128)} %constant.160.clone.1, s32[]{:T(128)} %constant.160.clone.1, s32[]{:T(128)} %constant.161.clone.1) | dynamic-update-slice | bytes 58372 | tf_op jit(solution)/shard_map/scatter-add | solution.py:160
  260.5 0.7 fusion.123
  261.2 5.1 collective-permute-start.6
  267.3 2.8 stack.217
  270.3 0.8 all_to_all.39
  271.1 7.6 %all-to-all-start.2 = ((f32[32,1,768]{2,1,0:T(1,128)}), f32[32,1,768]{2,1,0:T(1,128)S(1)}, u32[]{:S(2)}, u32[]{:S(2)}) async-start(f32[32,1,768]{2,1,0:T(1,128)} %all_to_all.39), calls=%async_computation.2 | async-start | bytes 196608 | tf_op jit(solution)/shard_map/all_to_all | solution.py:150
  278.7 1.3 collective-permute-start.7
  280.0 18.1 %all-reduce.10.cloned.1.call-done = (f32[64,256]{1,0:T(8,128)}, f32[256,64]{0,1:T(8,128)}) async-done(((f32[64,256]{1,0:T(8,128)}, f32[256,64]{0,1:T(8,128)}), (f32[64,256]{1,0:T(8,128)}, f32[256,64]{0,1:T(8,128)})) %all-reduce.10.cloned.1.call-update) | async-done | bytes 131088 | tf_op jit(solution)/shard_map/psum | solution.py:223
  298.2 0.9 slice_add_fusion.1
  299.8 0.7 copy.32
  300.5 13.5 %all-to-all-start.3 = ((f32[32,1,768]{2,1,0:T(1,128)}), f32[32,1,768]{2,1,0:T(1,128)S(1)}, u32[]{:S(2)}, u32[]{:S(2)}) async-start(f32[32,1,768]{2,1,0:T(1,128)} %copy.32), calls=%async_computation.3 | async-start | bytes 196608 | tf_op jit(solution)/shard_map/all_to_all | solution.py:151
  314.0 194.1 %all-reduce.8.cloned.1.call-done = (f32[64,256]{1,0:T(8,128)}, f32[256,64]{0,1:T(8,128)}) async-done(((f32[64,256]{1,0:T(8,128)}, f32[256,64]{0,1:T(8,128)}), (f32[64,256]{1,0:T(8,128)}, f32[256,64]{0,1:T(8,128)})) %all-reduce.8.cloned.1.call-update) | async-done | bytes 131088 | tf_op jit(solution)/shard_map/psum | solution.py:222
  508.1 1.5 broadcast_multiply_fusion
  509.6 1.5 broadcast_multiply_fusion.1
  511.6 1.0 select_add_fusion
  513.4 1.6 convert_reduce_fusion.1
  515.0 34.2 %all-reduce.3 = (f32[64,49]{0,1:T(8,128)S(1)}, f32[256]{0:T(256)S(1)}, f32[64]{0:T(128)S(1)}, f32[64]{0:T(128)S(1)}, f32[64]{0:T(128)S(1)}, /*index=5*/f32[64]{0:T(128)S(1)}, f32[64]{0:T(128)S(1)}) all-reduce(f32[64,49]{0,1:T(8,128)S(1)} %stack.217, f32[256]{0:T(256)S(1)} %copy-done.91, ...), channel_id=1, replica_groups=mesh['lat'=8,'lon'=32] {'lat'}, use_global_device_ids=true, to_apply=%region_53.54 | all-reduce | flops 3712 | bytes 29696 | tf_op jit(solution)/shard_map/psum | solution.py:223
  549.2 107.6 %all-reduce.1 = (f32[64,49]{0,1:T(8,128)S(1)}, f32[256]{0:T(256)S(1)}, f32[1,64]{1,0:T(1,128)S(1)}, f32[1,64]{1,0:T(1,128)S(1)}, f32[1,64]{1,0:T(1,128)S(1)}, /*index=5*/f32[1,64]{1,0:T(1,128)S(1)}, f32[1,64]{1,0:T(1,128)S(1)}) all-reduce(f32[64,49]{0,1:T(8,128)S(1)} %get-tuple-element.137, ...), channel_id=1, replica_groups=mesh['lat'=8,'lon'=32] {'lon'}, use_global_device_ids=true, to_apply=%region_54.55 | all-reduce | flops 3712 | bytes 29696 | tf_op jit(solution)/shard_map/psum | solution.py:222
  (252 shorter events, 10.4 us)
Async XLA Ops:
  7.2 95.8 %copy-start = (bf16[64,256]{1,0:T(8,128)(2,1)S(1)}, bf16[64,256]{1,0:T(8,128)(2,1)}, u32[]{:S(2)}) copy-start(bf16[64,256]{1,0:T(8,128)(2,1)} %param.27) | copy-start | bytes 98308
  7.2 31.7 %copy-start.10 = (bf16[64,32,128]{2,1,0:T(8,128)(2,1)S(1)}, bf16[64,32,128]{2,1,0:T(8,128)(2,1)}, u32[]{:S(2)}) copy-start(bf16[64,32,128]{2,1,0:T(8,128)(2,1)} %param.22) | copy-start | bytes 1572868
  8.3 38.9 %collective-permute-start = (f32[64,3,128]{2,1,0:T(4,128)S(1)}, f32[64,3,128]{2,1,0:T(4,128)S(1)}, u32[]{:S(2)}, u32[]{:S(2)}) collective-permute-start(f32[64,3,128]{2,1,0:T(4,128)S(1)} %get-tuple-element.165), channel_id=1, source_target_pairs={{0,32},{32,64},{64,96},{96,128},{128,160},{160,192},{192,224},{1,3... | collective-permute-start | bytes 294920 | tf_op jit(solution)/shard_map/ppermute | solution.py:19
  13.1 18.9 %all-to-all-start = ((f32[32,1,768]{2,1,0:T(1,128)}), f32[32,1,768]{2,1,0:T(1,128)S(1)}, u32[]{:S(2)}, u32[]{:S(2)}) async-start(f32[32,1,768]{2,1,0:T(1,128)} %all_to_all.38), calls=%async_computation | async-start | bytes 196608 | tf_op jit(solution)/shard_map/all_to_all | solution.py:150
  23.6 23.6 %collective-permute-start.1 = (f32[64,3,128]{2,1,0:T(4,128)S(1)}, f32[64,3,128]{2,1,0:T(4,128)S(1)}, u32[]{:S(2)}, u32[]{:S(2)}) collective-permute-start(f32[64,3,128]{2,1,0:T(4,128)S(1)} %get-tuple-element.164), channel_id=1, source_target_pairs={{32,0},{64,32},{96,64},{128,96},{160,128},{192,160},{224,192},{33,... | collective-permute-start | bytes 294920 | tf_op jit(solution)/shard_map/ppermute | solution.py:20
  32.8 13.7 %all-to-all-start.1 = ((f32[32,1,768]{2,1,0:T(1,128)}), f32[32,1,768]{2,1,0:T(1,128)S(1)}, u32[]{:S(2)}, u32[]{:S(2)}) async-start(f32[32,1,768]{2,1,0:T(1,128)} %copy.20), calls=%async_computation.1 | async-start | bytes 196608 | tf_op jit(solution)/shard_map/all_to_all | solution.py:151
  38.2 259.9 %all-reduce.10.cloned.1.call-start = ((), (), s32[]{:S(2)}) async-start(), calls=%async_computation.5 | async-start | bytes 262144 | tf_op jit(solution)/shard_map/psum | solution.py:223
  50.8 5.2 collective-permute-start.2
  53.2 4.4 collective-permute-start.3
  115.3 40.5 %copy-start.2 = (f32[8,8,32,128]{3,2,1,0:T(8,128)}, f32[8,8,32,128]{3,2,1,0:T(8,128)S(1)}, u32[]{:S(2)}) copy-start(f32[8,8,32,128]{3,2,1,0:T(8,128)S(1)} %copy.39) | copy-start | bytes 3145732
  123.3 28.6 %copy-start.93 = (f32[64]{0:T(128)S(1)}, f32[64]{0:T(128)}, u32[]{:S(2)}) copy-start(f32[64]{0:T(128)} %convert_element_type.92) | copy-start | bytes 772
  195.9 27.8 %collective-permute-start.4 = (f32[64,38,3]{0,1,2:T(8,128)}, f32[64,38,3]{0,1,2:T(8,128)}, u32[]{:S(2)}, u32[]{:S(2)}) collective-permute-start(f32[64,38,3]{0,1,2:T(8,128)} %copy.25), channel_id=1, source_target_pairs={{0,1},{1,2},{2,3},{3,4},{4,5},{5,6},{6,7},{7,8},{8,9},{9,10},{10,1... | collective-permute-start | bytes 87560 | tf_op jit(solution)/shard_map/ppermute | solution.py:19
  200.0 40.5 %collective-permute-start.5 = (f32[64,38,3]{0,1,2:T(8,128)}, f32[64,38,3]{0,1,2:T(8,128)S(1)}, u32[]{:S(2)}, u32[]{:S(2)}) collective-permute-start(f32[64,38,3]{0,1,2:T(8,128)} %copy.28), channel_id=1, source_target_pairs={{1,0},{2,1},{3,2},{4,3},{5,4},{6,5},{7,6},{8,7},{9,8},{10,9},{11,1... | collective-permute-start | bytes 87560 | tf_op jit(solution)/shard_map/ppermute | solution.py:20
  240.6 25.8 %copy-start.3 = (f32[8,8,32,128]{3,2,1,0:T(8,128)S(1)}, f32[8,8,32,128]{3,2,1,0:T(8,128)}, u32[]{:S(2)}) copy-start(f32[8,8,32,128]{3,2,1,0:T(8,128)} %copy-done.2) | copy-start | bytes 3145732
  242.1 24.8 %copy-start.49 = (f32[64]{0:T(128)S(1)}, f32[64]{0:T(128)}, u32[]{:S(2)}) copy-start(f32[64]{0:T(128)} %get-tuple-element.85) | copy-start | bytes 772
  242.1 24.8 %copy-start.50 = (f32[64]{0:T(128)S(1)}, f32[64]{0:T(128)}, u32[]{:S(2)}) copy-start(f32[64]{0:T(128)} %get-tuple-element.86) | copy-start | bytes 772
  242.1 24.8 %copy-start.51 = (f32[64]{0:T(128)S(1)}, f32[64]{0:T(128)}, u32[]{:S(2)}) copy-start(f32[64]{0:T(128)} %get-tuple-element.87) | copy-start | bytes 772
  242.1 24.8 %copy-start.52 = (f32[64]{0:T(128)S(1)}, f32[64]{0:T(128)}, u32[]{:S(2)}) copy-start(f32[64]{0:T(128)} %get-tuple-element.88) | copy-start | bytes 772
  242.1 24.8 %copy-start.53 = (f32[64]{0:T(128)S(1)}, f32[64]{0:T(128)}, u32[]{:S(2)}) copy-start(f32[64]{0:T(128)} %get-tuple-element.89) | copy-start | bytes 772
  242.2 24.8 %copy-start.54 = (f32[64]{0:T(128)S(1)}, f32[64]{0:T(128)}, u32[]{:S(2)}) copy-start(f32[64]{0:T(128)} %get-tuple-element.90) | copy-start | bytes 772
  242.2 24.8 %copy-start.55 = (f32[64]{0:T(128)S(1)}, f32[64]{0:T(128)}, u32[]{:S(2)}) copy-start(f32[64]{0:T(128)} %get-tuple-element.91) | copy-start | bytes 772
  242.2 24.8 %copy-start.56 = (f32[64]{0:T(128)S(1)}, f32[64]{0:T(128)}, u32[]{:S(2)}) copy-start(f32[64]{0:T(128)} %get-tuple-element.92) | copy-start | bytes 772
  242.2 24.8 %copy-start.57 = (f32[64]{0:T(128)S(1)}, f32[64]{0:T(128)}, u32[]{:S(2)}) copy-start(f32[64]{0:T(128)} %get-tuple-element.93) | copy-start | bytes 772
  242.2 24.8 %copy-start.58 = (f32[64]{0:T(128)S(1)}, f32[64]{0:T(128)}, u32[]{:S(2)}) copy-start(f32[64]{0:T(128)} %get-tuple-element.94) | copy-start | bytes 772
  242.2 24.8 %copy-start.59 = (f32[64]{0:T(128)S(1)}, f32[64]{0:T(128)}, u32[]{:S(2)}) copy-start(f32[64]{0:T(128)} %get-tuple-element.95) | copy-start | bytes 772
  242.2 24.8 %copy-start.60 = (f32[64]{0:T(128)S(1)}, f32[64]{0:T(128)}, u32[]{:S(2)}) copy-start(f32[64]{0:T(128)} %get-tuple-element.96) | copy-start | bytes 772
  242.2 24.8 %copy-start.61 = (f32[64]{0:T(128)S(1)}, f32[64]{0:T(128)}, u32[]{:S(2)}) copy-start(f32[64]{0:T(128)} %get-tuple-element.97) | copy-start | bytes 772
  242.2 24.8 %copy-start.62 = (f32[64]{0:T(128)S(1)}, f32[64]{0:T(128)}, u32[]{:S(2)}) copy-start(f32[64]{0:T(128)} %get-tuple-element.98) | copy-start | bytes 772
  242.2 24.8 %copy-start.63 = (f32[64]{0:T(128)S(1)}, f32[64]{0:T(128)}, u32[]{:S(2)}) copy-start(f32[64]{0:T(128)} %get-tuple-element.99) | copy-start | bytes 772
  242.3 24.8 %copy-start.64 = (f32[64]{0:T(128)S(1)}, f32[64]{0:T(128)}, u32[]{:S(2)}) copy-start(f32[64]{0:T(128)} %get-tuple-element.100) | copy-start | bytes 772
  242.3 24.8 %copy-start.65 = (f32[64]{0:T(128)S(1)}, f32[64]{0:T(128)}, u32[]{:S(2)}) copy-start(f32[64]{0:T(128)} %get-tuple-element.101) | copy-start | bytes 772
  242.3 24.8 %copy-start.66 = (f32[64]{0:T(128)S(1)}, f32[64]{0:T(128)}, u32[]{:S(2)}) copy-start(f32[64]{0:T(128)} %get-tuple-element.102) | copy-start | bytes 772
  242.3 24.8 %copy-start.67 = (f32[64]{0:T(128)S(1)}, f32[64]{0:T(128)}, u32[]{:S(2)}) copy-start(f32[64]{0:T(128)} %get-tuple-element.67) | copy-start | bytes 772
  242.3 24.8 %copy-start.68 = (f32[64]{0:T(128)S(1)}, f32[64]{0:T(128)}, u32[]{:S(2)}) copy-start(f32[64]{0:T(128)} %get-tuple-element.68) | copy-start | bytes 772
  242.3 24.8 %copy-start.69 = (f32[64]{0:T(128)S(1)}, f32[64]{0:T(128)}, u32[]{:S(2)}) copy-start(f32[64]{0:T(128)} %get-tuple-element.69) | copy-start | bytes 772
  242.3 24.8 %copy-start.70 = (f32[64]{0:T(128)S(1)}, f32[64]{0:T(128)}, u32[]{:S(2)}) copy-start(f32[64]{0:T(128)} %get-tuple-element.70) | copy-start | bytes 772
  242.3 24.8 %copy-start.71 = (f32[64]{0:T(128)S(1)}, f32[64]{0:T(128)}, u32[]{:S(2)}) copy-start(f32[64]{0:T(128)} %get-tuple-element.71) | copy-start | bytes 772
  242.3 24.8 %copy-start.72 = (f32[64]{0:T(128)S(1)}, f32[64]{0:T(128)}, u32[]{:S(2)}) copy-start(f32[64]{0:T(128)} %get-tuple-element.72) | copy-start | bytes 772
  242.3 24.8 %copy-start.73 = (f32[64]{0:T(128)S(1)}, f32[64]{0:T(128)}, u32[]{:S(2)}) copy-start(f32[64]{0:T(128)} %get-tuple-element.73) | copy-start | bytes 772
  242.4 24.8 %copy-start.74 = (f32[64]{0:T(128)S(1)}, f32[64]{0:T(128)}, u32[]{:S(2)}) copy-start(f32[64]{0:T(128)} %get-tuple-element.74) | copy-start | bytes 772
  242.4 24.8 %copy-start.75 = (f32[64]{0:T(128)S(1)}, f32[64]{0:T(128)}, u32[]{:S(2)}) copy-start(f32[64]{0:T(128)} %get-tuple-element.75) | copy-start | bytes 772
  242.4 24.8 %copy-start.76 = (f32[64]{0:T(128)S(1)}, f32[64]{0:T(128)}, u32[]{:S(2)}) copy-start(f32[64]{0:T(128)} %get-tuple-element.76) | copy-start | bytes 772
  242.4 24.8 %copy-start.77 = (f32[64]{0:T(128)S(1)}, f32[64]{0:T(128)}, u32[]{:S(2)}) copy-start(f32[64]{0:T(128)} %get-tuple-element.77) | copy-start | bytes 772
  242.4 24.8 %copy-start.78 = (f32[64]{0:T(128)S(1)}, f32[64]{0:T(128)}, u32[]{:S(2)}) copy-start(f32[64]{0:T(128)} %get-tuple-element.78) | copy-start | bytes 772
  242.4 24.8 %copy-start.79 = (f32[64]{0:T(128)S(1)}, f32[64]{0:T(128)}, u32[]{:S(2)}) copy-start(f32[64]{0:T(128)} %get-tuple-element.79) | copy-start | bytes 772
  242.4 24.8 %copy-start.80 = (f32[64]{0:T(128)S(1)}, f32[64]{0:T(128)}, u32[]{:S(2)}) copy-start(f32[64]{0:T(128)} %get-tuple-element.80) | copy-start | bytes 772
  242.4 24.8 %copy-start.81 = (f32[64]{0:T(128)S(1)}, f32[64]{0:T(128)}, u32[]{:S(2)}) copy-start(f32[64]{0:T(128)} %get-tuple-element.81) | copy-start | bytes 772
  242.4 24.8 %copy-start.82 = (f32[64]{0:T(128)S(1)}, f32[64]{0:T(128)}, u32[]{:S(2)}) copy-start(f32[64]{0:T(128)} %get-tuple-element.82) | copy-start | bytes 772
  242.4 24.8 %copy-start.83 = (f32[64]{0:T(128)S(1)}, f32[64]{0:T(128)}, u32[]{:S(2)}) copy-start(f32[64]{0:T(128)} %get-tuple-element.83) | copy-start | bytes 772
  242.5 24.8 %copy-start.84 = (f32[64]{0:T(128)S(1)}, f32[64]{0:T(128)}, u32[]{:S(2)}) copy-start(f32[64]{0:T(128)} %get-tuple-element.84) | copy-start | bytes 772
  242.5 24.8 %copy-start.89 = (f32[64]{0:T(128)S(1)}, f32[64]{0:T(128)}, u32[]{:S(2)}) copy-start(f32[64]{0:T(128)} %get-tuple-element.109) | copy-start | bytes 772
  242.5 24.8 %copy-start.90 = (f32[64]{0:T(128)S(1)}, f32[64]{0:T(128)}, u32[]{:S(2)}) copy-start(f32[64]{0:T(128)} %get-tuple-element.110) | copy-start | bytes 772
  261.2 36.9 %collective-permute-start.6 = (f32[64,3,128]{2,1,0:T(4,128)S(1)}, f32[64,3,128]{2,1,0:T(4,128)}, u32[]{:S(2)}, u32[]{:S(2)}) collective-permute-start(f32[64,3,128]{2,1,0:T(4,128)S(1)} %get-tuple-element.155), channel_id=1, source_target_pairs={{0,32},{32,64},{64,96},{96,128},{128,160},{160,192},{192,224},{1,3... | collective-permute-start | bytes 294920 | tf_op jit(solution)/shard_map/ppermute | solution.py:19
  266.9 11.8 %copy-start.12 = (f32[64,3,128]{2,1,0:T(4,128)S(1)}, f32[64,3,128]{2,1,0:T(4,128)}, u32[]{:S(2)}) copy-start(f32[64,3,128]{2,1,0:T(4,128)} %get-tuple-element.154) | copy-start | bytes 294916
  270.1 243.2 %copy-start.11 = (bf16[64,32,128]{2,1,0:T(8,128)(2,1)S(1)}, bf16[64,32,128]{2,1,0:T(8,128)(2,1)}, u32[]{:S(2)}) copy-start(bf16[64,32,128]{2,1,0:T(8,128)(2,1)} %param.33) | copy-start | bytes 1572868
  271.1 28.6 %all-to-all-start.2 = ((f32[32,1,768]{2,1,0:T(1,128)}), f32[32,1,768]{2,1,0:T(1,128)S(1)}, u32[]{:S(2)}, u32[]{:S(2)}) async-start(f32[32,1,768]{2,1,0:T(1,128)} %all_to_all.39), calls=%async_computation.2 | async-start | bytes 196608 | tf_op jit(solution)/shard_map/all_to_all | solution.py:150
  278.7 229.4 %all-reduce.8.cloned.1.call-start = ((), (), s32[]{:S(2)}) async-start(), calls=%async_computation.4 | async-start | bytes 262144 | tf_op jit(solution)/shard_map/psum | solution.py:222
  278.7 232.9 %collective-permute-start.7 = (f32[64,3,128]{2,1,0:T(4,128)S(1)}, f32[64,3,128]{2,1,0:T(4,128)}, u32[]{:S(2)}, u32[]{:S(2)}) collective-permute-start(f32[64,3,128]{2,1,0:T(4,128)S(1)} %copy-done.12), channel_id=1, source_target_pairs={{32,0},{64,32},{96,64},{128,96},{160,128},{192,160},{224,192},{33,... | collective-permute-start | bytes 294920 | tf_op jit(solution)/shard_map/ppermute | solution.py:20
  299.1 215.8 %copy-start.85 = (f32[64]{0:T(128)S(1)}, f32[64]{0:T(128)}, u32[]{:S(2)}) copy-start(f32[64]{0:T(128)} %reduce_sum.587) | copy-start | bytes 772
  299.1 215.8 %copy-start.86 = (f32[64]{0:T(128)S(1)}, f32[64]{0:T(128)}, u32[]{:S(2)}) copy-start(f32[64]{0:T(128)} %get-tuple-element.115) | copy-start | bytes 772
  299.2 215.8 %copy-start.87 = (f32[64]{0:T(128)S(1)}, f32[64]{0:T(128)}, u32[]{:S(2)}) copy-start(f32[64]{0:T(128)} %get-tuple-element.116) | copy-start | bytes 772
  299.2 215.8 %copy-start.88 = (f32[64]{0:T(128)S(1)}, f32[64]{0:T(128)}, u32[]{:S(2)}) copy-start(f32[64]{0:T(128)} %get-tuple-element.160) | copy-start | bytes 772
  299.2 215.8 %copy-start.91 = (f32[256]{0:T(256)S(1)}, f32[256]{0:T(256)}, u32[]{:S(2)}) copy-start(f32[256]{0:T(256)} %get-tuple-element.222) | copy-start | bytes 3076
  300.5 210.5 %all-to-all-start.3 = ((f32[32,1,768]{2,1,0:T(1,128)}), f32[32,1,768]{2,1,0:T(1,128)S(1)}, u32[]{:S(2)}, u32[]{:S(2)}) async-start(f32[32,1,768]{2,1,0:T(1,128)} %copy.32), calls=%async_computation.3 | async-start | bytes 196608 | tf_op jit(solution)/shard_map/all_to_all | solution.py:151
  (50 other events, 215.6 us)
Sparse Core Ops, SparseCore 0:
  212.6 85.5 all-reduce.9
  300.8 207.2 all-reduce.7
